TPU v7x, 32 devices: a whole 2x2x4 slice. The times are simulated.
32 devices in a mesh: groups: 2 (over x), scene: 16 (over z, y, core).
Axes of the slice: x: 2, y: 2, z: 4, core: 2. Of those that a mesh axis runs over, the one named last changes fastest.
Arguments:
- tokens: bfloat16 [32, 196, 768], P(('groups', 'scene')), parts along dimension 0, may hold values from -6 to 6
- qkv_weight: bfloat16 [768, 2304], replicated, may hold values from -0.21875 to 0.21875
- out_weight: bfloat16 [768, 768], replicated, may hold values from -0.21875 to 0.21875
- attn_gain: float32 [768], replicated, may hold values from 0.1 to 1.9
- head_gain: float32 [768], replicated, may hold values from 0.1 to 1.9
- head_weight: bfloat16 [768, 1024], replicated, may hold values from -0.21875 to 0.21875
- head_bias: float32 [1024], replicated, may hold values from -3 to 3
- pair_list: int32 [64, 2], P('groups'), parts along dimension 0, may hold values from 0 to 15, as said below
- pair_count: int32 [32], P('groups'), parts along dimension 0, may hold values from 1 to 2, as said below
Outputs:
- joined: float32 [32, 196, 768], P(('groups', 'scene')), parts along dimension 0
There are 2 independent parts, one for each index of `groups`. A program takes and returns all parts, laid end to end along the dimension named above; an argument that names none is the same for every part. Nothing has to cross between parts.
Inputs may be any that keep to these rules, and one draw needn't show every extreme that they name: `pair_list`: slot j of device d (row d * 2 + j) holds a pair whose first image is d + (j mod 1); its second image is owned by a device 1 to 2 places away along the scene axis taken as a cycle, image i being owned by device i. `pair_count`: entry d is the number of live slots of device d; slots from that number on are ignored. In every draw some device has exactly 2 and another exactly 1.
All inputs are finite; a program needn't handle non-finite values.
Results may differ from a plain program's by a relative error of at most 0.0045.
Values may be sent and summed in bfloat16 or wider, within the bound.
No kernel may reach another device: no remote copies, remote signals or barrier semaphores. Data moves between devices by JAX's collectives and lax.ppermute only.
A program may use at most 128 MiB of HBM per device.

v0:
```python
import functools

import jax
import jax.numpy as jnp
from jax import lax
from jax.experimental import pallas as pl
from jax.experimental.pallas import tpu as pltpu
from jax.sharding import PartitionSpec as P


HEADS = 12
TEMPER = 16.0
CONF_RANGE = 4.0
EPSILON = 1e-06
LANES = 128
MXU = 256

VMEM_SPEC = pl.BlockSpec(memory_space=pltpu.VMEM)
HBM_SPEC = pl.BlockSpec(memory_space=pltpu.HBM)


def in_hbm(value):
    return pltpu.with_memory_space_constraint(value, pltpu.HBM)


def round_up(value, step):
    return -(-value // step) * step


def layer_norm(values, gain_row):
    centred = values - jnp.mean(values, axis=-1, keepdims=True)
    spread = jnp.mean(centred * centred, axis=-1, keepdims=True)
    return centred * lax.rsqrt(spread + EPSILON) * gain_row


def matmul(left, right):
    return jnp.dot(left, right, preferred_element_type=jnp.float32)


def head_block(head_size):
    rows = lax.broadcasted_iota(jnp.int32, (MXU, MXU), 0) // head_size
    cols = lax.broadcasted_iota(jnp.int32, (MXU, MXU), 1) // head_size
    return jnp.where(rows == cols, 1.0 / head_size, 0.0).astype(jnp.bfloat16)


def head_unit(mixed, block):
    energy = matmul((mixed * mixed).astype(jnp.bfloat16), block)
    return (mixed * lax.rsqrt(energy + EPSILON)).astype(jnp.bfloat16)


def multiplicity(pair_list, pair_count, own, partner, slots):
    count = jnp.int32(0)
    for slot in range(slots):
        for first, second in ((own, partner), (partner, own)):
            live = slot < pair_count[first]
            hit = pair_list[1, first * slots + slot] == second
            count = count + jnp.where(jnp.logical_and(live, hit), 1, 0)
    return count


def attend(normed, q_ref, kv_ref, keys_scr, vals_scr, att_ref):
    tokens, width = normed.shape
    head_size = width // HEADS
    rows = q_ref.shape[1] // 2
    padded = keys_scr.shape[0]
    pairs = width // LANES
    low_head = lax.broadcasted_iota(jnp.int32, (1, LANES), 1) < head_size
    block = head_block(head_size)

    tail = tokens // 16 * 16
    keys_scr[tail:, :] = jnp.zeros((padded - tail, width), jnp.bfloat16)
    row = lax.broadcasted_iota(jnp.int32, (padded, LANES), 0)
    ones = jnp.where(row < tokens, 1.0, 0.0).astype(jnp.bfloat16)
    for pair in range(pairs):
        vals_scr[pair, tail:, :LANES] = jnp.zeros((padded - tail, LANES), jnp.bfloat16)
        vals_scr[pair, :, LANES:] = ones

    for start in range(0, width, MXU):
        keys_scr[:tokens, start : start + MXU] = head_unit(matmul(normed, kv_ref[:, start : start + MXU]), block)
        value = matmul(normed, kv_ref[:, width + start : width + start + MXU]).astype(jnp.bfloat16)
        for half in range(MXU // LANES):
            vals_scr[start // LANES + half, :tokens, :LANES] = value[:, half * LANES : (half + 1) * LANES]
    for pair in range(pairs):
        scores = lax.dot_general(
            q_ref[pair],
            keys_scr[:, pair * LANES : (pair + 1) * LANES],
            (((1,), (1,)), ((), ())),
            preferred_element_type=jnp.float32,
        )
        exponent = jnp.exp(scores * (TEMPER / head_size)).astype(jnp.bfloat16)
        mixed = matmul(exponent, vals_scr[pair])
        top = jnp.where(low_head, mixed[:tokens, :LANES], mixed[rows : rows + tokens, :LANES])
        norm = jnp.where(low_head, mixed[:tokens, LANES:], mixed[rows : rows + tokens, LANES:])
        att_ref[:, pair * LANES : (pair + 1) * LANES] = (top / norm).astype(jnp.bfloat16)


def finish(attended, count_row, own_ref, out_ref, head_ref, gains_ref, bias_ref, emit):
    pixels = head_ref.shape[1] // 4
    mixed = own_ref[...].astype(jnp.float32) + matmul(attended, out_ref[...])
    head_in = layer_norm(mixed, gains_ref[1:2, :]).astype(jnp.bfloat16)
    conf = matmul(head_in, head_ref[:, 3 * pixels :]) + bias_ref[:, 3 * pixels :]
    conf = conf.astype(jnp.bfloat16).astype(jnp.float32)
    weight = jnp.exp(CONF_RANGE * jnp.tanh(conf / CONF_RANGE)) * count_row
    for part in range(3):
        cols = slice(part * pixels, (part + 1) * pixels)
        xyz = matmul(head_in, head_ref[:, cols]) + bias_ref[:, cols]
        emit(part, cols, weight, weight * xyz.astype(jnp.bfloat16).astype(jnp.float32))


def view_scratch(tokens, width):
    padded, pairs = round_up(tokens, MXU), width // LANES
    return [
        pltpu.VMEM((padded, width), jnp.bfloat16),
        pltpu.VMEM((pairs, padded, MXU), jnp.bfloat16),
        pltpu.VMEM((tokens, width), jnp.bfloat16),
    ]


def first_kernel(
    scene_size,
    slots,
    offsets_of,
    tokens_hbm,
    qkv_hbm,
    attn_gain_hbm,
    head_gain_hbm,
    bias_hbm,
    list_hbm,
    count_hbm,
    own_ref,
    normed_ref,
    kv_ref,
    gains_ref,
    bias_ref,
    counts_ref,
    q_ref,
    wq_scr,
    list_smem,
    count_smem,
    sems,
):
    tokens, width = own_ref.shape
    head_size = width // HEADS
    rows = q_ref.shape[1] // 2
    first_cols = [slice(start, start + MXU) for start in range(0, width, MXU)]
    plan = [
        (tokens_hbm.at[0], own_ref),
        (attn_gain_hbm, gains_ref.at[0]),
        *((qkv_hbm.at[:, cols], wq_scr.at[:, cols]) for cols in first_cols),
        (list_hbm, list_smem),
        (count_hbm, count_smem),
        (head_gain_hbm, gains_ref.at[1]),
        (bias_hbm, bias_ref.at[0]),
        (qkv_hbm.at[:, width : 2 * width], kv_ref.at[:, :width]),
        (qkv_hbm.at[:, 2 * width :], kv_ref.at[:, width:]),
    ]
    copies = [pltpu.make_async_copy(source, target, sems.at[at]) for at, (source, target) in enumerate(plan)]
    for copy in copies:
        copy.start()
    low_head = lax.broadcasted_iota(jnp.int32, (1, LANES), 1) < head_size
    block = head_block(head_size)
    tail = tokens // 16 * 16
    for half in range(2):
        q_ref[:, half * rows + tail : (half + 1) * rows, :] = jnp.zeros((q_ref.shape[0], rows - tail, LANES), jnp.bfloat16)
    for copy in copies[:2]:
        copy.wait()
    normed_ref[...] = layer_norm(own_ref[...].astype(jnp.float32), gains_ref[0:1, :]).astype(jnp.bfloat16)
    normed = normed_ref[...]
    for at, cols in enumerate(first_cols):
        copies[2 + at].wait()
        unit = head_unit(matmul(normed, wq_scr[:, cols]), block)
        for half in range(MXU // LANES):
            pair = cols.start // LANES + half
            piece = unit[:, half * LANES : (half + 1) * LANES]
            zero = jnp.zeros_like(piece)
            q_ref[pair, :tokens, :] = jnp.where(low_head, piece, zero)
            q_ref[pair, rows : rows + tokens, :] = jnp.where(low_head, zero, piece)
    for copy in copies[2 + len(first_cols) :]:
        copy.wait()
    position = lax.axis_index("scene")
    for at, offset in enumerate(offsets_of(position)):
        partner = lax.rem(position + offset + scene_size, scene_size)
        count = multiplicity(list_smem, count_smem, position, partner, slots).astype(jnp.float32)
        counts_ref[at] = jnp.full(counts_ref.shape[1:], count, jnp.float32)


def is_live(counts_ref, at):
    return jnp.max(counts_ref[at]) > 0


def mate_kernel(gains_ref, counts_ref, q_ref, kv_ref, partner_ref, att_ref, keys_scr, vals_scr):
    position = lax.axis_index("scene")

    @pl.when(jnp.logical_or(position >= 2, jnp.logical_and(position == 1, is_live(counts_ref, 0))))
    def _():
        normed = layer_norm(partner_ref[...].astype(jnp.float32), gains_ref[0:1, :]).astype(jnp.bfloat16)
        attend(normed, q_ref, kv_ref, keys_scr, vals_scr, att_ref)


def mate_maps_kernel(own_ref, gains_ref, bias_ref, counts_ref, q_ref, kv_ref, out_ref, head_ref, partner_ref, *refs):
    _, sums_ref, weights_ref, att_ref, keys_scr, vals_scr = refs
    position = lax.axis_index("scene")
    live = is_live(counts_ref, 0)
    runs = jnp.logical_or(position >= 2, live)

    def emit(part, cols, weight, weighted):
        sums_ref[:, cols] = weighted
        if part == 0:
            weights_ref[...] = weight

    @pl.when(jnp.logical_and(position == 0, live))
    def _():
        normed = layer_norm(partner_ref[...].astype(jnp.float32), gains_ref[0:1, :]).astype(jnp.bfloat16)
        attend(normed, q_ref, kv_ref, keys_scr, vals_scr, att_ref)

    @pl.when(runs)
    def _():
        finish(att_ref[...], counts_ref[0, 0:1, 0:1], own_ref, out_ref, head_ref, gains_ref, bias_ref, emit)

    @pl.when(jnp.logical_not(runs))
    def _():
        sums_ref[...] = jnp.zeros_like(sums_ref)
        weights_ref[...] = jnp.zeros_like(weights_ref)


def view_kernel(at, own_ref, gains_ref, bias_ref, counts_ref, q_ref, kv_ref, out_ref, head_ref, partner_ref, *refs):
    sums_in, weights_in, sums_ref, weights_ref, keys_scr, vals_scr, att_scr = refs

    def emit(part, cols, weight, weighted):
        sums_ref[:, cols] = sums_in[:, cols] + weighted
        if part == 2:
            weights_ref[...] = weights_in[...] + weight

    @pl.when(is_live(counts_ref, at))
    def _():
        normed = layer_norm(partner_ref[...].astype(jnp.float32), gains_ref[0:1, :]).astype(jnp.bfloat16)
        attend(normed, q_ref, kv_ref, keys_scr, vals_scr, att_scr)
        finish(att_scr[...], counts_ref[at, 0:1, 0:1], own_ref, out_ref, head_ref, gains_ref, bias_ref, emit)


def last_kernel(at, own_ref, gains_ref, bias_ref, counts_ref, q_ref, kv_ref, out_ref, head_ref, normed_ref, *refs):
    sums_in, weights_in, joined_hbm, keys_scr, vals_scr, att_scr, joined_scr, sem = refs

    def store(cols, ratio):
        lines = sums_in.shape[1] // LANES
        for line in range(ratio.shape[1] // LANES):
            rows = pl.ds(cols.start // LANES + line, ratio.shape[0], stride=lines)
            joined_scr[rows, :] = ratio[:, line * LANES : (line + 1) * LANES]

    def emit(part, cols, weight, weighted):
        store(cols, (sums_in[:, cols] + weighted) / (weights_in[...] + weight))

    live = is_live(counts_ref, at)

    @pl.when(live)
    def _():
        attend(normed_ref[...], q_ref, kv_ref, keys_scr, vals_scr, att_scr)
        finish(att_scr[...], counts_ref[at, 0:1, 0:1], own_ref, out_ref, head_ref, gains_ref, bias_ref, emit)

    @pl.when(jnp.logical_not(live))
    def _():
        pixels = weights_in.shape[1]
        for part in range(3):
            cols = slice(part * pixels, (part + 1) * pixels)
            store(cols, sums_in[:, cols] / weights_in[...])

    copy = pltpu.make_async_copy(joined_scr, joined_hbm, sem)
    copy.start()
    copy.wait()


def per_device(
    tokens, qkv_weight, out_weight, attn_gain, head_gain, head_weight, head_bias, pair_list, pair_count
):
    scene_size = lax.axis_size("scene")
    _, token_count, width = tokens.shape
    slots = pair_list.shape[0] // scene_size
    columns = head_weight.shape[1]
    pixels = columns // 4
    f32, bf16 = jnp.float32, jnp.bfloat16
    own = tokens[0]

    def moved(value, target_of):
        return lax.ppermute(value, "scene", [(s, target_of(s) % scene_size) for s in range(scene_size)])

    def mate_of(s):
        return s ^ 1

    def offsets_of(position):
        to_mate = 1 - 2 * lax.rem(position, 2)
        return (to_mate, -to_mate, 2 * to_mate, -2 * to_mate)

    sums = jax.ShapeDtypeStruct((token_count, 3 * pixels), f32)
    weights = jax.ShapeDtypeStruct((token_count, pixels), f32)
    params = pltpu.CompilerParams(vmem_limit_bytes=24 * 2**20)
    cost = pl.CostEstimate(flops=4 * token_count * width * width * 2, bytes_accessed=2**20, transcendentals=0)

    alpha = moved(own, lambda s: s + 1 if s % 2 else s - 1)
    mate = moved(own, mate_of)
    first_shapes = (
        jax.ShapeDtypeStruct((token_count, width), bf16),
        jax.ShapeDtypeStruct((token_count, width), bf16),
        jax.ShapeDtypeStruct((width, 2 * width), bf16),
        jax.ShapeDtypeStruct((2, width), f32),
        jax.ShapeDtypeStruct((1, columns), f32),
        jax.ShapeDtypeStruct((4, 8, LANES), f32),
        jax.ShapeDtypeStruct((width // LANES, 2 * round_up(token_count, 16), LANES), bf16),
    )
    own_vmem, normed, kv_vmem, gains, bias, counts, queries = pl.pallas_call(
        functools.partial(first_kernel, scene_size, slots, offsets_of),
        out_shape=first_shapes,
        in_specs=[HBM_SPEC] * 7,
        out_specs=tuple(VMEM_SPEC for _ in first_shapes),
        scratch_shapes=[
            pltpu.VMEM((width, width), bf16),
            pltpu.SMEM((2, pair_list.shape[0]), jnp.int32),
            pltpu.SMEM(pair_count.shape, jnp.int32),
            pltpu.SemaphoreType.DMA((8 + width // MXU,)),
        ],
        compiler_params=params,
        cost_estimate=cost,
        name="load_queries",
    )(
        in_hbm(tokens),
        *(in_hbm(value) for value in (qkv_weight, attn_gain, head_gain, head_bias)),
        in_hbm(pair_list.T),
        in_hbm(pair_count),
    )

    def kernel(body, operands, in_specs, out_shape, out_spec, scratch, aliases={}):
        return pl.pallas_call(
            body,
            out_shape=out_shape,
            in_specs=in_specs,
            out_specs=[out_spec] * len(out_shape),
            scratch_shapes=scratch,
            input_output_aliases=aliases,
            compiler_params=params,
            cost_estimate=cost,
        )(*operands)

    scratch = view_scratch(token_count, width)
    (attended,) = kernel(
        mate_kernel,
        (gains, counts, queries, kv_vmem, mate),
        [VMEM_SPEC] * 5,
        [jax.ShapeDtypeStruct((token_count, width), bf16)],
        VMEM_SPEC,
        scratch[:2],
    )
    normed, attended = lax.optimization_barrier((normed, attended))
    beta = moved(normed, lambda s: s - 2 if s % 2 else s + 2)
    common = (own_vmem, gains, bias, counts, queries, kv_vmem, out_weight, head_weight)
    *totals, _ = kernel(
        mate_maps_kernel,
        (*common, mate, attended),
        [VMEM_SPEC] * 10,
        (sums, weights, jax.ShapeDtypeStruct((token_count, width), bf16)),
        VMEM_SPEC,
        scratch[:2],
        {9: 2},
    )
    alpha, *totals = lax.optimization_barrier((alpha, *totals))
    swapped = moved(alpha, mate_of)
    for at, partner in ((1, alpha), (2, swapped)):
        totals = kernel(
            functools.partial(view_kernel, at),
            (*common, partner, *totals),
            [VMEM_SPEC] * 11,
            (sums, weights),
            VMEM_SPEC,
            scratch,
            {9: 0, 10: 1},
        )
    joined_shape = jax.ShapeDtypeStruct((token_count * 3 * pixels // LANES, LANES), f32)
    (joined,) = kernel(
        functools.partial(last_kernel, 3),
        (*common, beta, *totals),
        [VMEM_SPEC] * 11,
        (joined_shape,),
        HBM_SPEC,
        scratch + [pltpu.VMEM(joined_shape.shape, f32), pltpu.SemaphoreType.DMA],
    )
    return joined.reshape(1, token_count, 3 * pixels)


def solution(mesh):
    return jax.shard_map(
        per_device,
        mesh=mesh,
        in_specs=(
            P(("groups", "scene"), None, None),
            P(),
            P(),
            P(),
            P(),
            P(),
            P(),
            P("groups", None),
            P("groups"),
        ),
        out_specs=P(("groups", "scene"), None, None),
        check_vma=False,
    )
```

profile of v0, /device:TPU:12, one launch (start us, length us, event | category | flops | bytes accessed | tf_op | source)
XLA Modules:
  0.0 24.0 jit_solution(9968179549726909632)
XLA Ops:
  0.0 0.0 collective-permute-start
  0.0 0.6 %collective-permute-start.2 = (bf16[196,768]{1,0:T(8,128)(2,1)}, bf16[196,768]{1,0:T(8,128)(2,1)S(1)}, u32[]{:S(2)}, u32[]{:S(2)}) collective-permute-start(bf16[196,768]{1,0:T(8,128)(2,1)} %bitcast.4), channel_id=1, source_target_pairs={{0,15},{1,2},{2,1},{3,4},{4,3},{5,6},{6,5},{7,8},{8,7},{9,10},{10,... | collective-permute-start | bytes 903176 | tf_op jit(solution)/shard_map/ppermute | solution.py:284
  0.6 2.8 %load_queries.1 = (bf16[196,768]{1,0:T(8,128)(2,1)S(1)}, bf16[196,768]{1,0:T(8,128)(2,1)S(1)}, bf16[768,1536]{1,0:T(8,128)(2,1)S(1)}, f32[2,768]{1,0:T(2,128)S(1...) custom-call(bf16[1,196,768]{2,1,0:T(8,128)(2,1)} %tokens_hbm.1, ...), custom_call_target="tpu_custom_call" | custom-call | flops 924844032 | bytes 1048576 | tf_op jit(solution)/shard_map/load_queries/pallas_call | solution.py:309
  3.4 0.0 copy-start
  3.4 0.0 copy-start.1
  3.4 0.0 collective-permute-done.partner_ref
  3.4 2.0 %shard_map.91.refs_0_ = bf16[196,768]{1,0:T(8,128)(2,1)S(1)} custom-call(f32[2,768]{1,0:T(2,128)S(1)} %get-tuple-element.24.gains_ref, f32[4,8,128]{2,1,0:T(8,128)S(1)} %get-tuple-element.26.counts_ref, bf16[6,416,128]{2,1,0:T(8,128)(2,1)S(1)} %get-tuple-element.27.q_ref, bf16[768,1536]{1,0:T(8,128)(2,1)S(1)} %get-tuple-element.28.kv_ref, ...), custom_call_target="tpu_custom_call" | custom-call | flops 924844032 | bytes 1048576 | tf_op jit(solution)/shard_map/pallas_call | solution.py:331
  5.5 0.0 copy-done
  5.5 0.0 copy-done.1
  5.5 1.3 %shard_map.92 = (f32[196,768]{1,0:T(8,128)S(1)}, f32[196,256]{1,0:T(8,128)S(1)}, bf16[196,768]{1,0:T(8,128)(2,1)S(1)}) custom-call(bf16[196,768]{1,0:T(8,128)(2,1)S(1)} %get-tuple-element.23.own_ref, f32[2,768]{1,0:T(2,128)S(1)} %get-tuple-element.24.gains_ref, f32[1,1024]{1,0:T(1,128)S(1)} %get-tuple-element.25.bias_ref, ...), custom_call_target="tpu_custom_call", output_to_operand_aliasing={{2}: (9, {})} | custom-call | flops 924844032 | bytes 1048576 | tf_op jit(solution)/shard_map/pallas_call | solution.py:331
  6.8 3.0 %collective-permute-done.2.partner_ref = bf16[196,768]{1,0:T(8,128)(2,1)S(1)} collective-permute-done((bf16[196,768]{1,0:T(8,128)(2,1)}, bf16[196,768]{1,0:T(8,128)(2,1)S(1)}, u32[]{:S(2)}, u32[]{:S(2)}) %collective-permute-start.2) | collective-permute-done | bytes 301088 | tf_op jit(solution)/shard_map/ppermute | solution.py:284
  9.8 0.0 collective-permute-start.3
  9.8 2.0 %collective-permute-start.1 = (bf16[196,768]{1,0:T(8,128)(2,1)S(1)}, bf16[196,768]{1,0:T(8,128)(2,1)S(1)}, u32[]{:S(2)}, u32[]{:S(2)}) collective-permute-start(bf16[196,768]{1,0:T(8,128)(2,1)S(1)} %get-tuple-element.30), channel_id=1, source_target_pairs={{0,2},{1,15},{2,4},{3,1},{4,6},{5,3},{6,8},{7,5},{8,10},{9,7},{10,... | collective-permute-start | bytes 903176 | tf_op jit(solution)/shard_map/ppermute | solution.py:284
  11.8 3.1 %shard_map.93 = (f32[196,768]{1,0:T(8,128)S(1)}, f32[196,256]{1,0:T(8,128)S(1)}) custom-call(bf16[196,768]{1,0:T(8,128)(2,1)S(1)} %get-tuple-element.23.own_ref, f32[2,768]{1,0:T(2,128)S(1)} %get-tuple-element.24.gains_ref, f32[1,1024]{1,0:T(1,128)S(1)} %get-tuple-element.25.bias_ref, ...), custom_call_target="tpu_custom_call", output_to_operand_aliasing={{0}: (9, {}), {1}: (10, {})} | custom-call | flops 924844032 | bytes 1048576 | tf_op jit(solution)/shard_map/pallas_call | solution.py:331
  14.9 0.0 collective-permute-done.3.partner_ref
  14.9 3.1 %shard_map.94 = (f32[196,768]{1,0:T(8,128)S(1)}, f32[196,256]{1,0:T(8,128)S(1)}) custom-call(bf16[196,768]{1,0:T(8,128)(2,1)S(1)} %get-tuple-element.23.own_ref, f32[2,768]{1,0:T(2,128)S(1)} %get-tuple-element.24.gains_ref, f32[1,1024]{1,0:T(1,128)S(1)} %get-tuple-element.25.bias_ref, ...), custom_call_target="tpu_custom_call", output_to_operand_aliasing={{0}: (9, {}), {1}: (10, {})} | custom-call | flops 924844032 | bytes 1048576 | tf_op jit(solution)/shard_map/pallas_call | solution.py:331
  18.1 1.9 %collective-permute-done.1.normed_ref = bf16[196,768]{1,0:T(8,128)(2,1)S(1)} collective-permute-done((bf16[196,768]{1,0:T(8,128)(2,1)S(1)}, bf16[196,768]{1,0:T(8,128)(2,1)S(1)}, u32[]{:S(2)}, u32[]{:S(2)}) %collective-permute-start.1) | collective-permute-done | bytes 301088 | tf_op jit(solution)/shard_map/ppermute | solution.py:284
  19.9 3.9 %shard_map.95 = f32[1176,128]{1,0:T(8,128)} custom-call(bf16[196,768]{1,0:T(8,128)(2,1)S(1)} %get-tuple-element.23.own_ref, f32[2,768]{1,0:T(2,128)S(1)} %get-tuple-element.24.gains_ref, f32[1,1024]{1,0:T(1,128)S(1)} %get-tuple-element.25.bias_ref, f32[4,8,128]{2,1,0:T(8,128)S(1)} %get-tuple-element.26.counts_ref, ...), custom_call_target="tpu_custom_call" | custom-call | flops 924844032 | bytes 1048576 | tf_op jit(solution)/shard_map/pallas_call | solution.py:331
Async XLA Ops:
  0.0 3.4 %collective-permute-start = (bf16[196,768]{1,0:T(8,128)(2,1)}, bf16[196,768]{1,0:T(8,128)(2,1)S(1)}, u32[]{:S(2)}, u32[]{:S(2)}) collective-permute-start(bf16[196,768]{1,0:T(8,128)(2,1)} %bitcast.3), channel_id=1, source_target_pairs={{0,1},{1,0},{2,3},{3,2},{4,5},{5,4},{6,7},{7,6},{8,9},{9,8},{10,11... | collective-permute-start | bytes 903176 | tf_op jit(solution)/shard_map/ppermute | solution.py:284
  0.0 9.8 %collective-permute-start.2 = (bf16[196,768]{1,0:T(8,128)(2,1)}, bf16[196,768]{1,0:T(8,128)(2,1)S(1)}, u32[]{:S(2)}, u32[]{:S(2)}) collective-permute-start(bf16[196,768]{1,0:T(8,128)(2,1)} %bitcast.4), channel_id=1, source_target_pairs={{0,15},{1,2},{2,1},{3,4},{4,3},{5,6},{6,5},{7,8},{8,7},{9,10},{10,... | collective-permute-start | bytes 903176 | tf_op jit(solution)/shard_map/ppermute | solution.py:284
  3.4 2.1 %copy-start = (bf16[768,1024]{1,0:T(8,128)(2,1)S(1)}, bf16[768,1024]{1,0:T(8,128)(2,1)}, u32[]{:S(2)}) copy-start(bf16[768,1024]{1,0:T(8,128)(2,1)} %head_ref.7) | copy-start | bytes 4718596
  3.4 2.1 %copy-start.1 = (bf16[768,768]{1,0:T(8,128)(2,1)S(1)}, bf16[768,768]{1,0:T(8,128)(2,1)}, u32[]{:S(2)}) copy-start(bf16[768,768]{1,0:T(8,128)(2,1)} %out_ref.7) | copy-start | bytes 3538948
  9.8 5.2 %collective-permute-start.3 = (bf16[196,768]{1,0:T(8,128)(2,1)S(1)}, bf16[196,768]{1,0:T(8,128)(2,1)S(1)}, u32[]{:S(2)}, u32[]{:S(2)}) collective-permute-start(bf16[196,768]{1,0:T(8,128)(2,1)S(1)} %collective-permute-done.2.partner_ref), channel_id=1, source_target_pairs={{0,1},{1,0},{2,3},{3,2},{4,5},{5,4},{6,7},{7,6},{8,9},{9,8},{10,11... | collective-permute-start | bytes 903176 | tf_op jit(solution)/shard_map/ppermute | solution.py:284
  9.8 10.1 %collective-permute-start.1 = (bf16[196,768]{1,0:T(8,128)(2,1)S(1)}, bf16[196,768]{1,0:T(8,128)(2,1)S(1)}, u32[]{:S(2)}, u32[]{:S(2)}) collective-permute-start(bf16[196,768]{1,0:T(8,128)(2,1)S(1)} %get-tuple-element.30), channel_id=1, source_target_pairs={{0,2},{1,15},{2,4},{3,1},{4,6},{5,3},{6,8},{7,5},{8,10},{9,7},{10,... | collective-permute-start | bytes 903176 | tf_op jit(solution)/shard_map/ppermute | solution.py:284
where the time goes:
time: 24.2 us; the launch traced here: 24 us
  Pallas kernels  16.2 us (67%)
  waiting for transfers between devices  4.86 us (20%)
  starting transfers between devices  2.65 us (11%)
  between operations  0.25 us (1%)
    pallas_call x5, Pallas kernels, kernel(): pl.pallas_call(body, out_shape=out_shape, in_specs=in_specs, out_specs=[o...  13.5 us
    ppermute x4, waiting for transfers between devices, moved(): lax.ppermute(value, 'scene', [(s, target_of(s) % scene_size) for s in ran...  4.86 us
    pallas_call x1, Pallas kernels, per_device(): pl.pallas_call(functools.partial(first_kernel, scene_size, slots, offsets...  2.76 us
    ppermute x4, starting transfers between devices, moved(): lax.ppermute(value, 'scene', [(s, target_of(s) % scene_size) for s in ran...  2.65 us
  transfers between devices with their start and end apart: 4, of which 2 were waited for; matrix products, arithmetic and copies ran while one was open for 0% of the time, Pallas kernels for 51%

commit v1 on v0

--- a/solution.py
+++ b/solution.py
@@ -185,33 +185,27 @@
 
 
 def is_live(counts_ref, at):
-    return jnp.max(counts_ref[at]) > 0
+    return jnp.max(counts_ref[at, 0:1, 0:1]) > 0
+
+
+def mate_runs(counts_ref):
+    return jnp.logical_or(is_live(counts_ref, 0), lax.axis_index("scene") >= 2)
 
 
 def mate_kernel(gains_ref, counts_ref, q_ref, kv_ref, partner_ref, att_ref, keys_scr, vals_scr):
-    position = lax.axis_index("scene")
-
-    @pl.when(jnp.logical_or(position >= 2, jnp.logical_and(position == 1, is_live(counts_ref, 0))))
+    @pl.when(mate_runs(counts_ref))
     def _():
         normed = layer_norm(partner_ref[...].astype(jnp.float32), gains_ref[0:1, :]).astype(jnp.bfloat16)
         attend(normed, q_ref, kv_ref, keys_scr, vals_scr, att_ref)
 
 
-def mate_maps_kernel(own_ref, gains_ref, bias_ref, counts_ref, q_ref, kv_ref, out_ref, head_ref, partner_ref, *refs):
-    _, sums_ref, weights_ref, att_ref, keys_scr, vals_scr = refs
-    position = lax.axis_index("scene")
-    live = is_live(counts_ref, 0)
-    runs = jnp.logical_or(position >= 2, live)
-
+def mate_maps_kernel(own_ref, gains_ref, bias_ref, counts_ref, att_ref, out_ref, head_ref, sums_ref, weights_ref):
     def emit(part, cols, weight, weighted):
         sums_ref[:, cols] = weighted
         if part == 0:
             weights_ref[...] = weight
 
-    @pl.when(jnp.logical_and(position == 0, live))
-    def _():
-        normed = layer_norm(partner_ref[...].astype(jnp.float32), gains_ref[0:1, :]).astype(jnp.bfloat16)
-        attend(normed, q_ref, kv_ref, keys_scr, vals_scr, att_ref)
+    runs = mate_runs(counts_ref)
 
     @pl.when(runs)
     def _():
@@ -350,18 +344,17 @@
     )
     normed, attended = lax.optimization_barrier((normed, attended))
     beta = moved(normed, lambda s: s - 2 if s % 2 else s + 2)
-    common = (own_vmem, gains, bias, counts, queries, kv_vmem, out_weight, head_weight)
-    *totals, _ = kernel(
+    totals = kernel(
         mate_maps_kernel,
-        (*common, mate, attended),
-        [VMEM_SPEC] * 10,
-        (sums, weights, jax.ShapeDtypeStruct((token_count, width), bf16)),
+        (own_vmem, gains, bias, counts, attended, out_weight, head_weight),
+        [VMEM_SPEC] * 7,
+        (sums, weights),
         VMEM_SPEC,
-        scratch[:2],
-        {9: 2},
+        [],
     )
     alpha, *totals = lax.optimization_barrier((alpha, *totals))
     swapped = moved(alpha, mate_of)
+    common = (own_vmem, gains, bias, counts, queries, kv_vmem, out_weight, head_weight)
     for at, partner in ((1, alpha), (2, swapped)):
         totals = kernel(
             functools.partial(view_kernel, at),

time: 24.2 us -> 23.7 us (0.979)
  the two profiles are of different devices: /device:TPU:12 before, /device:TPU:20 now
where the time goes in v1:
time: 23.7 us; the launch traced here: 23.6 us
  Pallas kernels  15.7 us (66%)
  waiting for transfers between devices  5.1 us (22%)
  starting transfers between devices  2.65 us (11%)
    pallas_call x5, Pallas kernels, kernel(): pl.pallas_call(body, out_shape=out_shape, in_specs=in_specs, out_specs=[o...  13 us
    ppermute x4, waiting for transfers between devices, moved(): lax.ppermute(value, 'scene', [(s, target_of(s) % scene_size) for s in ran...  5.1 us
    pallas_call x1, Pallas kernels, per_device(): pl.pallas_call(functools.partial(first_kernel, scene_size, slots, offsets...  2.77 us
    ppermute x4, starting transfers between devices, moved(): lax.ppermute(value, 'scene', [(s, target_of(s) % scene_size) for s in ran...  2.65 us
  transfers between devices with their start and end apart: 4, of which 2 were waited for; matrix products, arithmetic and copies ran while one was open for 0% of the time, Pallas kernels for 51%

profile of v1, /device:TPU:20, one launch (start us, length us, event | category | flops | bytes accessed | tf_op | source)
XLA Modules:
  0.0 23.6 jit_solution(14624143616005128399)
XLA Ops:
  0.0 0.0 collective-permute-start
  0.0 0.6 %collective-permute-start.2 = (bf16[196,768]{1,0:T(8,128)(2,1)}, bf16[196,768]{1,0:T(8,128)(2,1)S(1)}, u32[]{:S(2)}, u32[]{:S(2)}) collective-permute-start(bf16[196,768]{1,0:T(8,128)(2,1)} %bitcast.4), channel_id=1, source_target_pairs={{0,15},{1,2},{2,1},{3,4},{4,3},{5,6},{6,5},{7,8},{8,7},{9,10},{10,... | collective-permute-start | bytes 903176 | tf_op jit(solution)/shard_map/ppermute | solution.py:278
  0.6 2.8 %load_queries.1 = (bf16[196,768]{1,0:T(8,128)(2,1)S(1)}, bf16[196,768]{1,0:T(8,128)(2,1)S(1)}, bf16[768,1536]{1,0:T(8,128)(2,1)S(1)}, f32[2,768]{1,0:T(2,128)S(1...) custom-call(bf16[1,196,768]{2,1,0:T(8,128)(2,1)} %tokens_hbm.1, ...), custom_call_target="tpu_custom_call" | custom-call | flops 924844032 | bytes 1048576 | tf_op jit(solution)/shard_map/load_queries/pallas_call | solution.py:303
  3.4 0.0 copy-start
  3.4 0.0 copy-start.1
  3.4 0.0 collective-permute-done.partner_ref
  3.4 2.0 %shard_map.91.att_ref = bf16[196,768]{1,0:T(8,128)(2,1)S(1)} custom-call(f32[2,768]{1,0:T(2,128)S(1)} %get-tuple-element.24.gains_ref, f32[4,8,128]{2,1,0:T(8,128)S(1)} %get-tuple-element.26.counts_ref, bf16[6,416,128]{2,1,0:T(8,128)(2,1)S(1)} %get-tuple-element.27.q_ref, bf16[768,1536]{1,0:T(8,128)(2,1)S(1)} %get-tuple-element.28.kv_ref, ...), custom_call_target="tpu_custom_call" | custom-call | flops 924844032 | bytes 1048576 | tf_op jit(solution)/shard_map/pallas_call | solution.py:325
  5.4 0.0 copy-done
  5.4 0.0 copy-done.1
  5.4 1.2 %shard_map.92 = (f32[196,768]{1,0:T(8,128)S(1)}, f32[196,256]{1,0:T(8,128)S(1)}) custom-call(bf16[196,768]{1,0:T(8,128)(2,1)S(1)} %get-tuple-element.23.own_ref, f32[2,768]{1,0:T(2,128)S(1)} %get-tuple-element.24.gains_ref, f32[1,1024]{1,0:T(1,128)S(1)} %get-tuple-element.25.bias_ref, f32[4,8,128]{2,1,0:T(8,128)S(1)} %get-tuple-element.26.counts_ref, ...), custom_call_target="tpu_custom_call" | custom-call | flops 924844032 | bytes 1048576 | tf_op jit(solution)/shard_map/pallas_call | solution.py:325
  6.6 3.1 %collective-permute-done.2.partner_ref = bf16[196,768]{1,0:T(8,128)(2,1)S(1)} collective-permute-done((bf16[196,768]{1,0:T(8,128)(2,1)}, bf16[196,768]{1,0:T(8,128)(2,1)S(1)}, u32[]{:S(2)}, u32[]{:S(2)}) %collective-permute-start.2) | collective-permute-done | bytes 301088 | tf_op jit(solution)/shard_map/ppermute | solution.py:278
  9.8 0.0 collective-permute-start.3
  9.8 2.0 %collective-permute-start.1 = (bf16[196,768]{1,0:T(8,128)(2,1)S(1)}, bf16[196,768]{1,0:T(8,128)(2,1)S(1)}, u32[]{:S(2)}, u32[]{:S(2)}) collective-permute-start(bf16[196,768]{1,0:T(8,128)(2,1)S(1)} %get-tuple-element.30), channel_id=1, source_target_pairs={{0,2},{1,15},{2,4},{3,1},{4,6},{5,3},{6,8},{7,5},{8,10},{9,7},{10,... | collective-permute-start | bytes 903176 | tf_op jit(solution)/shard_map/ppermute | solution.py:278
  11.8 3.1 %shard_map.93 = (f32[196,768]{1,0:T(8,128)S(1)}, f32[196,256]{1,0:T(8,128)S(1)}) custom-call(bf16[196,768]{1,0:T(8,128)(2,1)S(1)} %get-tuple-element.23.own_ref, f32[2,768]{1,0:T(2,128)S(1)} %get-tuple-element.24.gains_ref, f32[1,1024]{1,0:T(1,128)S(1)} %get-tuple-element.25.bias_ref, ...), custom_call_target="tpu_custom_call", output_to_operand_aliasing={{0}: (9, {}), {1}: (10, {})} | custom-call | flops 924844032 | bytes 1048576 | tf_op jit(solution)/shard_map/pallas_call | solution.py:325
  14.9 0.0 collective-permute-done.3.partner_ref
  14.9 3.1 %shard_map.94 = (f32[196,768]{1,0:T(8,128)S(1)}, f32[196,256]{1,0:T(8,128)S(1)}) custom-call(bf16[196,768]{1,0:T(8,128)(2,1)S(1)} %get-tuple-element.23.own_ref, f32[2,768]{1,0:T(2,128)S(1)} %get-tuple-element.24.gains_ref, f32[1,1024]{1,0:T(1,128)S(1)} %get-tuple-element.25.bias_ref, ...), custom_call_target="tpu_custom_call", output_to_operand_aliasing={{0}: (9, {}), {1}: (10, {})} | custom-call | flops 924844032 | bytes 1048576 | tf_op jit(solution)/shard_map/pallas_call | solution.py:325
  18.0 2.0 %collective-permute-done.1.normed_ref = bf16[196,768]{1,0:T(8,128)(2,1)S(1)} collective-permute-done((bf16[196,768]{1,0:T(8,128)(2,1)S(1)}, bf16[196,768]{1,0:T(8,128)(2,1)S(1)}, u32[]{:S(2)}, u32[]{:S(2)}) %collective-permute-start.1) | collective-permute-done | bytes 301088 | tf_op jit(solution)/shard_map/ppermute | solution.py:278
  19.9 3.7 %shard_map.95 = f32[1176,128]{1,0:T(8,128)} custom-call(bf16[196,768]{1,0:T(8,128)(2,1)S(1)} %get-tuple-element.23.own_ref, f32[2,768]{1,0:T(2,128)S(1)} %get-tuple-element.24.gains_ref, f32[1,1024]{1,0:T(1,128)S(1)} %get-tuple-element.25.bias_ref, f32[4,8,128]{2,1,0:T(8,128)S(1)} %get-tuple-element.26.counts_ref, ...), custom_call_target="tpu_custom_call" | custom-call | flops 924844032 | bytes 1048576 | tf_op jit(solution)/shard_map/pallas_call | solution.py:325
Async XLA Ops:
  0.0 3.4 %collective-permute-start = (bf16[196,768]{1,0:T(8,128)(2,1)}, bf16[196,768]{1,0:T(8,128)(2,1)S(1)}, u32[]{:S(2)}, u32[]{:S(2)}) collective-permute-start(bf16[196,768]{1,0:T(8,128)(2,1)} %bitcast.3), channel_id=1, source_target_pairs={{0,1},{1,0},{2,3},{3,2},{4,5},{5,4},{6,7},{7,6},{8,9},{9,8},{10,11... | collective-permute-start | bytes 903176 | tf_op jit(solution)/shard_map/ppermute | solution.py:278
  0.0 9.8 %collective-permute-start.2 = (bf16[196,768]{1,0:T(8,128)(2,1)}, bf16[196,768]{1,0:T(8,128)(2,1)S(1)}, u32[]{:S(2)}, u32[]{:S(2)}) collective-permute-start(bf16[196,768]{1,0:T(8,128)(2,1)} %bitcast.4), channel_id=1, source_target_pairs={{0,15},{1,2},{2,1},{3,4},{4,3},{5,6},{6,5},{7,8},{8,7},{9,10},{10,... | collective-permute-start | bytes 903176 | tf_op jit(solution)/shard_map/ppermute | solution.py:278
  3.4 2.0 %copy-start = (bf16[768,1024]{1,0:T(8,128)(2,1)S(1)}, bf16[768,1024]{1,0:T(8,128)(2,1)}, u32[]{:S(2)}) copy-start(bf16[768,1024]{1,0:T(8,128)(2,1)} %head_ref.7) | copy-start | bytes 4718596
  3.4 2.0 %copy-start.1 = (bf16[768,768]{1,0:T(8,128)(2,1)S(1)}, bf16[768,768]{1,0:T(8,128)(2,1)}, u32[]{:S(2)}) copy-start(bf16[768,768]{1,0:T(8,128)(2,1)} %out_ref.7) | copy-start | bytes 3538948
  9.8 5.1 %collective-permute-start.3 = (bf16[196,768]{1,0:T(8,128)(2,1)S(1)}, bf16[196,768]{1,0:T(8,128)(2,1)S(1)}, u32[]{:S(2)}, u32[]{:S(2)}) collective-permute-start(bf16[196,768]{1,0:T(8,128)(2,1)S(1)} %collective-permute-done.2.partner_ref), channel_id=1, source_target_pairs={{0,1},{1,0},{2,3},{3,2},{4,5},{5,4},{6,7},{7,6},{8,9},{9,8},{10,11... | collective-permute-start | bytes 903176 | tf_op jit(solution)/shard_map/ppermute | solution.py:278
  9.8 10.1 %collective-permute-start.1 = (bf16[196,768]{1,0:T(8,128)(2,1)S(1)}, bf16[196,768]{1,0:T(8,128)(2,1)S(1)}, u32[]{:S(2)}, u32[]{:S(2)}) collective-permute-start(bf16[196,768]{1,0:T(8,128)(2,1)S(1)} %get-tuple-element.30), channel_id=1, source_target_pairs={{0,2},{1,15},{2,4},{3,1},{4,6},{5,3},{6,8},{7,5},{8,10},{9,7},{10,... | collective-permute-start | bytes 903176 | tf_op jit(solution)/shard_map/ppermute | solution.py:278
